TPU v7x, 128 devices: a whole 4x4x4 slice. The times are simulated.
128 devices in a mesh: dp: 16 (over x_lo, z, core), loop: 8 (over x_hi, y).
Axes of the slice: x: 4 (x_hi: 2, x_lo: 2; x = x_hi * 2 + x_lo), y: 4, z: 4, core: 2. Of those that a mesh axis runs over, the one named last changes fastest.
Arguments:
- crop_tokens: bfloat16 [8192, 64, 1152], P(('dp', 'loop')), may hold values from -6 to 6
- crop_lengths: int32 [128, 64], P(('dp', 'loop')), may hold values from 1 to 64, 3072 in all within a row
- crop_owner: int32 [8192, 1], P(('dp', 'loop')), may hold values from 0 to 15; in each aligned block of 64 rows (0 to 63, 64 to 127, ...) at most 8 rows name the same one
- crop_slot: int32 [8192], P(('dp', 'loop')), may hold values from 0 to 31
- base_tokens: bfloat16 [4096, 32, 1152], P(('dp', 'loop')), may hold values from -1024 to 1024
- key_probe: bfloat16 [1152, 16], replicated, may hold values from -1 to 1
- value_weight: bfloat16 [1152, 1152], replicated, may hold values from -0.1875 to 0.1875
- out_weight: bfloat16 [1152, 1152], replicated, may hold values from -0.1875 to 0.1875
- text_embed: bfloat16 [4096, 1152], P(('dp', 'loop')), may hold values from -6 to 6
- pair_labels: int32 [4096], P(('dp', 'loop')), may hold values from 0 to 63
- logit_scale: float32 [1], replicated, may hold values from 2 to 8
- logit_bias: float32 [1], replicated, may hold values from -4 to -1
Outputs:
- image_embed: bfloat16 [4096, 1152], P(('dp', 'loop'))
- image_grad: float32 [4096, 1152], P(('dp', 'loop'))
- text_grad: float32 [4096, 1152], P(('dp', 'loop'))
Inputs may be any that keep to these rules, and one draw needn't show every extreme that they name: `crop_owner`: at most 8 of the crops of one device name the same owner, and in every draw the crops of some device name one owner exactly 8 times. `crop_lengths`: the lengths of one device's crops sum to 3072 and the longest is exactly 64.
All inputs are finite; a program needn't handle non-finite values.
Results may differ from a plain program's by a relative error of at most 0.01.
Values may be sent and summed in bfloat16 or wider, within the bound.
No kernel may reach another device: no remote copies, remote signals or barrier semaphores. Data moves between devices by JAX's collectives and lax.ppermute only.
A program may use at most 192 MiB of HBM per device.

v0:
```python
import math
import jax
import jax.numpy as jnp
from jax import lax
from jax.sharding import PartitionSpec as P

very_low = -1e30
norm_eps = 1e-06
highest = lax.Precision.HIGHEST


def crop_partial(tokens, lengths, key_probe, value_weight):
    lead_shape = tokens.shape[:-2]
    crop_width = tokens.shape[-2]
    model_width = tokens.shape[-1]
    head_count = key_probe.shape[1]
    head_dim = model_width // head_count
    flat_rows = tokens.reshape(-1, model_width)
    scores = jnp.dot(flat_rows, key_probe, preferred_element_type=jnp.float32) / math.sqrt(head_dim)
    scores = scores.reshape(lead_shape + (crop_width, head_count))
    position = lax.broadcasted_iota(jnp.int32, lead_shape + (crop_width,), len(lead_shape))
    is_valid = (position < lengths[..., None])[..., None]
    masked = jnp.where(is_valid, scores, very_low)
    maxima = jnp.max(masked, axis=-2)
    weight = jnp.where(is_valid, jnp.exp(masked - maxima[..., None, :]), 0.0)
    totals = jnp.sum(weight, axis=-2)
    mixed = jnp.einsum("...kh,...kd->...hd", weight, tokens.astype(jnp.float32), precision=highest)
    value_heads = value_weight.astype(jnp.float32).reshape(model_width, head_count, head_dim)
    projected = jnp.einsum("...hd,dhe->...he", mixed, value_heads, precision=highest)
    return (projected.reshape(lead_shape + (model_width,)), maxima, totals)


def merge_parts(base_parts, arrived_parts, img_count):
    base_sum, base_max, base_total = base_parts
    mixed_sum, maxima, totals, slot_ids = arrived_parts
    slot_count, model_width = mixed_sum.shape
    head_count = maxima.shape[1]
    member = slot_ids[:, None] == lax.broadcasted_iota(jnp.int32, (1, img_count), 1)
    candidates = jnp.where(member[:, :, None], maxima[:, None, :], very_low)
    joint_max = jnp.maximum(base_max, jnp.max(candidates, axis=0))
    member_float = member.astype(jnp.float32)
    joint_at = jnp.dot(member_float, joint_max, precision=highest)
    rescale = jnp.exp(maxima - joint_at)
    base_rescale = jnp.exp(base_max - joint_max)
    scaled = (mixed_sum.reshape(slot_count, head_count, -1) * rescale[:, :, None]).reshape(
        slot_count, model_width
    )
    base_scaled = base_sum.reshape(img_count, head_count, -1) * base_rescale[:, :, None]
    collected = lax.dot_general(member_float, scaled, (((0,), (0,)), ((), ())), precision=highest)
    collected_total = lax.dot_general(
        member_float, totals * rescale, (((0,), (0,)), ((), ())), precision=highest
    )
    denominator = base_total * base_rescale + collected_total
    pooled = (base_scaled + collected.reshape(img_count, head_count, -1)) / denominator[:, :, None]
    return pooled.reshape(img_count, model_width).astype(jnp.bfloat16)


def unit_rows(matrix):
    return (matrix * lax.rsqrt(jnp.sum(matrix * matrix, axis=1, keepdims=True) + norm_eps)).astype(
        jnp.bfloat16
    )


def make_tile(image_rows, text_rows, row_labels, column_labels, scale_value, bias_value):
    logits = (
        scale_value
        * jnp.einsum("id,jd->ij", image_rows, text_rows, preferred_element_type=jnp.float32)
        + bias_value
    )
    target_sign = jnp.where(row_labels[:, None] == column_labels[None, :], 1.0, -1.0)
    return (scale_value * (-target_sign * jax.nn.sigmoid(-target_sign * logits))).astype(
        jnp.bfloat16
    )


def tile_terms(image_unit, text_block, block_labels, own_labels, scale_value, bias_value):
    grad_tile = make_tile(image_unit, text_block, own_labels, block_labels, scale_value, bias_value)
    image_term = jnp.dot(grad_tile, text_block, preferred_element_type=jnp.float32)
    text_term = jnp.einsum("ij,id->jd", grad_tile, image_unit, preferred_element_type=jnp.float32)
    return (image_term, text_term)


def per_device(
    crop_tokens,
    crop_lengths,
    crop_owner,
    crop_slot,
    base_tokens,
    key_probe,
    value_weight,
    out_weight,
    text_embed,
    pair_labels,
    logit_scale,
    logit_bias,
):
    owners = lax.axis_size("dp")
    crop_total = crop_tokens.shape[0]
    crop_width = crop_tokens.shape[1]
    model_width = crop_tokens.shape[2]
    img_count = base_tokens.shape[0]
    capacity = max(2, (2 * crop_total + owners - 1) // owners)
    slot_count = owners * capacity
    lengths = crop_lengths.reshape(-1)
    owner_ids = crop_owner[:, 0]
    member = (owner_ids[:, None] == lax.broadcasted_iota(jnp.int32, (1, owners), 1)).astype(
        jnp.int32
    )
    running = jnp.cumsum(member, axis=0)
    send_rank = jnp.sum(member * running, axis=1) - 1
    send_index = owner_ids * capacity + send_rank
    slot_ids = (
        jnp.zeros((slot_count,), jnp.int32).at[send_index].set(crop_slot).reshape(owners, capacity)
    )
    send_tokens = (
        jnp.zeros((slot_count, crop_width, model_width), jnp.bfloat16)
        .at[send_index]
        .set(crop_tokens)
    )
    send_lengths = jnp.zeros((slot_count,), jnp.int32).at[send_index].set(lengths)
    arrived_tokens = lax.all_to_all(
        send_tokens.reshape(owners, capacity, crop_width, model_width),
        "dp",
        split_axis=0,
        concat_axis=0,
        tiled=True,
    )
    arrived_lengths = lax.all_to_all(
        send_lengths.reshape(owners, capacity), "dp", split_axis=0, concat_axis=0, tiled=True
    )
    arrived_slots = lax.all_to_all(slot_ids, "dp", split_axis=0, concat_axis=0, tiled=True)
    mixed_sum, maxima, totals = crop_partial(
        arrived_tokens, arrived_lengths, key_probe, value_weight
    )
    received = (mixed_sum, maxima, totals, arrived_slots)
    flat_parts = tuple(
        (
            received_item.reshape((slot_count,) + received_item.shape[2:])
            for received_item in received
        )
    )
    base_lengths = jnp.full((img_count,), base_tokens.shape[1], jnp.int32)
    base_parts = crop_partial(base_tokens, base_lengths, key_probe, value_weight)
    pooled = merge_parts(base_parts, flat_parts, img_count)
    features = jnp.dot(pooled, out_weight, preferred_element_type=jnp.float32)
    image_embed = features.astype(jnp.bfloat16)
    image_unit = unit_rows(features)
    text_unit = unit_rows(text_embed.astype(jnp.float32))
    scale_value = logit_scale[0]
    bias_value = logit_bias[0]
    text_block = lax.all_gather(text_unit, "loop", axis=0, tiled=True)
    block_labels = lax.all_gather(pair_labels, "loop", axis=0, tiled=True)
    image_term, text_term = tile_terms(
        image_unit, text_block, block_labels, pair_labels, scale_value, bias_value
    )
    text_grad = lax.psum_scatter(
        text_term.astype(jnp.bfloat16), "loop", scatter_dimension=0, tiled=True
    ).astype(jnp.float32)
    return (image_embed, image_term, text_grad)


def solution(mesh):
    return jax.shard_map(
        per_device,
        mesh=mesh,
        in_specs=(
            P(("dp", "loop"), None, None),
            P(("dp", "loop"), None),
            P(("dp", "loop"), None),
            P(("dp", "loop")),
            P(("dp", "loop"), None, None),
            P(),
            P(),
            P(),
            P(("dp", "loop"), None),
            P(("dp", "loop")),
            P(),
            P(),
        ),
        out_specs=(P(("dp", "loop"), None), P(("dp", "loop"), None), P(("dp", "loop"), None)),
        check_vma=False,
    )
```

profile of v0, /device:TPU:0, one launch (start us, length us, event | category | flops | bytes accessed | tf_op | source)
XLA Modules:
  0.0 538.3 jit_solution(3503626312159067026)
XLA Ops:
  7.2 0.0 copy-start
  7.2 0.9 fusion.41
  8.1 0.1 reduce_window_sum.11
  8.2 0.8 select_reduce_fusion.1
  9.0 0.7 fusion.48
  9.7 0.9 scatter_custom_fusion.1
  10.6 0.7 all_to_all.17
  11.3 6.5 %all-to-all-start.1 = ((s32[16,1,8]{2,1,0:T(1,128)}), s32[16,1,8]{2,1,0:T(1,128)S(1)}, u32[]{:S(2)}, u32[]{:S(2)}) async-start(s32[16,1,8]{2,1,0:T(1,128)} %bitcast.8), calls=%async_computation.1 | async-start | bytes 16384 | tf_op jit(solution)/shard_map/all_to_all | solution.py:128
  17.7 0.9 scatter_custom_fusion
  18.6 0.7 all_to_all.15
  19.3 4.4 all-to-all-done.1
  23.7 3.5 all-to-all-start
  27.2 7.2 %broadcast_in_dim.92 = bf16[128,64,1152]{2,1,0:T(8,128)(2,1)} broadcast(bf16[]{:T(256)} %constant.10.clone.1), dimensions={} | broadcast | bytes 18874370 | tf_op jit(solution)/shard_map/broadcast_in_dim | solution.py:116
  34.4 23.5 %scatter_fusion = bf16[128,64,1152]{2,1,0:T(8,128)(2,1)} fusion(bf16[128,64,1152]{2,1,0:T(8,128)(2,1)} %broadcast_in_dim.92, s32[64]{0:T(128)S(1)} %fusion.48, bf16[64,64,1152]{2,1,0:T(8,128)(2,1)} %param.12), kind=kCustom, calls=%fused_computation.2 | custom fusion | bytes 28311808 | tf_op jit(solution)/shard_map/scatter | solution.py:118
  57.9 5.8 %all-to-all-start.2 = ((bf16[16,8,64,1152]{3,2,1,0:T(8,128)(2,1)}), bf16[16,8,64,1152]{3,2,1,0:T(8,128)(2,1)}, u32[]{:S(2)}, u32[]{:S(2)}) async-start(bf16[16,8,64,1152]{3,2,1,0:T(8,128)(2,1)} %bitcast.60), calls=%async_computation.2 | async-start | bytes 37748736 | tf_op jit(solution)/shard_map/all_to_all | solution.py:121
  63.7 0.0 reduce-scatter.2.cloned.1.call-start
  63.8 2.4 convolution_multiply_fusion.1
  66.1 0.1 reshape.114
  66.3 0.3 fusion.32
  66.6 0.1 copy.77
  66.6 0.2 copy-done.5
  66.8 0.3 fusion.33
  67.1 0.1 copy.83
  67.2 5.3 copy.67
  73.8 0.6 dynamic-slice
  75.1 0.2 dynamic-update-slice
  75.3 285.2 %all-reduce = s32[256]{0:T(256)} all-reduce(s32[256]{0:T(256)S(1)} %dynamic-update-slice), channel_id=1, replica_groups=mesh['dp'=16,'loop'=8] {'loop'}, use_global_device_ids=true, to_apply=%add | all-reduce | flops 256 | bytes 2048
  360.5 0.1 fusion.35
  360.6 0.1 fusion.36
  360.7 35.4 %all_gather.7 = bf16[256,1152]{1,0:T(8,128)(2,1)S(1)} all-gather(bf16[32,1152]{1,0:T(8,128)(2,1)S(1)} %fusion.36), channel_id=1, replica_groups=mesh['dp'=16,'loop'=8] {'loop'}, dimensions={0}, use_global_device_ids=true | all-gather | bytes 663552 | tf_op jit(solution)/shard_map/all_gather | solution.py:151
  396.1 4.4 fusion.34
  400.6 0.5 broadcast.92
  401.1 0.7 reduce.3
  401.7 0.1 eq.51
  401.8 0.1 iota_compare_fusion
  401.9 12.1 %convolution_multiply_fusion = f32[8192,16]{0,1:T(8,128)} fusion(bf16[8192,1152]{1,0:T(8,128)(2,1)} %bitcast.11, bf16[1152,16]{0,1:T(8,128)(2,1)} %param.17), kind=kOutput, calls=%fused_computation.5 | convolution fusion | flops 302120960 | bytes 19435520 | tf_op jit(solution)/shard_map/dot_general | solution.py:19
  414.1 2.4 reshape.119
  416.5 2.0 fusion.25
  418.6 0.2 select_reduce_fusion
  418.8 0.1 copy.76
  418.8 0.1 fusion.24
  419.0 2.4 fusion.26
  421.4 0.1 copy.84
  421.4 0.9 mul.78
  422.3 2.1 copy.81
  424.4 12.4 %fusion.27 = f32[16,8,16,1152]{3,2,1,0:T(8,128)S(1)} fusion(bf16[16,8,64,1152]{3,2,1,0:T(8,128)(2,1)} %all-to-all-done.2, f32[16,8,64,16]{2,1,0,3:T(8,128)} %reshape.119, f32[16,8,16]{2,1,0:T(8,128)S(1)} %fusion.25, pred[16,8,64]{2,1,0:T(8,128)(4,1)S(1)} %iota_compare_fusion), kind=kOutput, calls=%fused_computation.33 | convolution fusion | flops 1812332544 | bytes 28852224 | tf_op jit(solution)/shard_map/...kh,...kd->...hd/dot_general | solution.py:27
  436.9 7.0 %fusion.4 = f32[16,8,16,72]{3,1,0,2:T(8,128)S(1)} fusion(bf16[1152,16,72,1]{0,2,3,1:T(8,128)(2,1)S(1)} %bitcast.62, f32[16,8,16,1152]{3,2,1,0:T(8,128)S(1)} %fusion.27), kind=kOutput, calls=%fused_computation.9 | convolution fusion | flops 2038431744 | bytes 12681216 | tf_op jit(solution)/shard_map/...hd,dhe->...he/dot_general | solution.py:29
  443.9 1.6 copy.79
  445.5 2.4 reshape_reshape_reshape.3
  447.9 2.1 multiply_bitcast_fusion
  450.0 2.1 copy.82
  452.1 0.1 convolution_add_fusion.1
  452.2 5.3 fusion.10
  457.6 0.0 copy-start.6
  457.6 0.9 fusion.14
  458.5 0.1 copy.85
  458.5 0.2 convert_element_type.37
  458.7 1.3 multiply_reduce_fusion
  460.0 0.3 fusion.23
  460.4 1.2 convolution_convert_fusion
  461.5 0.0 reduce-scatter.2.cloned.1.call-update
  461.6 0.9 fusion.57
  462.4 67.5 %reduce-scatter.2.cloned.1.call-done = bf16[32,1152]{1,0:T(8,128)(2,1)} async-done(((bf16[256,1152]{1,0:T(8,128)(2,1)}), bf16[32,1152]{1,0:T(8,128)(2,1)}) %reduce-scatter.2.cloned.1.call-update) | async-done | bytes 73744 | tf_op jit(solution)/shard_map/reduce_scatter | solution.py:156
  529.9 1.6 convert_element_type.44
  (26 shorter events, 0.1 us)
Async XLA Ops:
  7.2 451.5 %copy-start = (bf16[1152,1152]{1,0:T(8,128)(2,1)S(1)}, bf16[1152,1152]{1,0:T(8,128)(2,1)}, u32[]{:S(2)}) copy-start(bf16[1152,1152]{1,0:T(8,128)(2,1)} %param.19) | copy-start | bytes 7962628
  11.3 12.5 %all-to-all-start.1 = ((s32[16,1,8]{2,1,0:T(1,128)}), s32[16,1,8]{2,1,0:T(1,128)S(1)}, u32[]{:S(2)}, u32[]{:S(2)}) async-start(s32[16,1,8]{2,1,0:T(1,128)} %bitcast.8), calls=%async_computation.1 | async-start | bytes 16384 | tf_op jit(solution)/shard_map/all_to_all | solution.py:128
  23.7 34.1 %all-to-all-start = ((s32[16,1,8]{2,1,0:T(1,128)}), s32[16,1,8]{2,1,0:T(1,128)S(1)}, u32[]{:S(2)}, u32[]{:S(2)}) async-start(s32[16,1,8]{2,1,0:T(1,128)} %bitcast.6), calls=%async_computation | async-start | bytes 16384 | tf_op jit(solution)/shard_map/all_to_all | solution.py:131
  57.9 5.9 %copy-start.4 = (bf16[1152,16]{0,1:T(8,128)(2,1)S(1)}, bf16[1152,16]{0,1:T(8,128)(2,1)}, u32[]{:S(2)}) copy-start(bf16[1152,16]{0,1:T(8,128)(2,1)} %param.17) | copy-start | bytes 110596
  57.9 344.1 %all-to-all-start.2 = ((bf16[16,8,64,1152]{3,2,1,0:T(8,128)(2,1)}), bf16[16,8,64,1152]{3,2,1,0:T(8,128)(2,1)}, u32[]{:S(2)}, u32[]{:S(2)}) async-start(bf16[16,8,64,1152]{3,2,1,0:T(8,128)(2,1)} %bitcast.60), calls=%async_computation.2 | async-start | bytes 37748736 | tf_op jit(solution)/shard_map/all_to_all | solution.py:121
  63.7 466.2 %reduce-scatter.2.cloned.1.call-start = ((), (), s32[]{:S(2)}) async-start(), calls=%async_computation.4 | async-start | bytes 663552 | tf_op jit(solution)/shard_map/reduce_scatter | solution.py:156
  66.3 0.5 copy-start.5
  67.2 6.6 %copy-start.9 = (u32[128]{0:T(128)S(1)}, u32[128]{0:T(128)}, u32[]{:S(2)}) copy-start(u32[128]{0:T(128)} %constant.46) | copy-start | bytes 1540
  67.2 7.9 %copy-start.7 = (s32[32]{0:T(128)S(1)}, s32[32]{0:T(128)}, u32[]{:S(2)}) copy-start(s32[32]{0:T(128)} %param.21) | copy-start | bytes 388
  67.2 293.3 %copy-start.3 = (bf16[32,1152]{1,0:T(8,128)(2,1)S(1)}, bf16[32,1152]{1,0:T(8,128)(2,1)}, u32[]{:S(2)}) copy-start(bf16[32,1152]{1,0:T(8,128)(2,1)} %param.20) | copy-start | bytes 221188
  424.4 12.5 %copy-start.1 = (bf16[1152,1152]{0,1:T(8,128)(2,1)S(1)}, bf16[1152,1152]{0,1:T(8,128)(2,1)}, u32[]{:S(2)}) copy-start(bf16[1152,1152]{0,1:T(8,128)(2,1)} %copy.67) | copy-start | bytes 7962628
  452.2 5.4 copy-start.2
  457.6 2.5 copy-start.6
  457.6 2.5 copy-start.8
Sparse Core Ops, SparseCore 0:
  461.7 68.1 reduce-scatter.1
where the time goes:
time: 540 us; the launch traced here: 538 us
  blocking collectives  321 us (59%)
  waiting for transfers between devices  71.9 us (13%)
  local copies, waits for them, and re-layouts  53.1 us (10%)
  matrix products  48.5 us (9%)
  between operations  16.3 us (3%)
  starting transfers between devices  15.8 us (3%)
  other arithmetic  12.2 us (2%)
    unnamed x1, blocking collectives  285 us
    reduce_scatter x1, waiting for transfers between devices, per_device(): lax.psum_scatter(text_term.astype(jnp.bfloat16), 'loop', scatter_dimensio...  67.5 us
    all_gather x1, blocking collectives, per_device(): text_block = lax.all_gather(text_unit, 'loop', axis=0, tiled=True)  35.4 us
    scatter x1, local copies, waits for them, and re-layouts, per_device(): send_tokens = jnp.zeros((slot_count, crop_width, model_width), jnp.bfloat...  23.5 us
    dot_general x2, matrix products, crop_partial(): jnp.einsum('...kh,...kd->...hd', weight, tokens.astype(jnp.float32), prec...  16.9 us
    dot_general x2, matrix products, crop_partial(): jnp.dot(flat_rows, key_probe, preferred_element_type=jnp.float32)  14.5 us
    dot_general x2, matrix products, crop_partial(): jnp.einsum('...hd,dhe->...he', mixed, value_heads, precision=highest)  12.3 us
  transfers between devices with their start and end apart: 4, of which 2 were waited for; matrix products, arithmetic and copies ran while one was open for 9% of the time, Pallas kernels for 0%

commit v1 on v0

--- a/solution.py
+++ b/solution.py
@@ -148,7 +148,9 @@
     text_unit = unit_rows(text_embed.astype(jnp.float32))
     scale_value = logit_scale[0]
     bias_value = logit_bias[0]
-    text_block = lax.all_gather(text_unit, "loop", axis=0, tiled=True)
+    text_block = jnp.concatenate(
+        lax.all_to_all(jnp.stack([text_unit] * lax.axis_size("loop")), "loop", 0, 0), axis=0
+    )
     block_labels = lax.all_gather(pair_labels, "loop", axis=0, tiled=True)
     image_term, text_term = tile_terms(
         image_unit, text_block, block_labels, pair_labels, scale_value, bias_value

time: 540 us -> 512 us (0.948)
  blocking collectives: 321 us -> 285 us
    all_gather x1 -> x0, blocking collectives: 35.4 us -> none  [per_device(): text_block = lax.all_gather(text_unit, 'loop', axis=0, tiled=True)]
  transfers between devices with their start and end apart: 4 -> 5, of which waited for: 2 -> 2; matrix products, arithmetic and copies ran while one was open for 9% -> 21% of each run, Pallas kernels for 0% -> 0%
where the time goes in v1:
time: 512 us; the launch traced here: 511 us
  blocking collectives  285 us (56%)
  waiting for transfers between devices  74.5 us (15%)
  local copies, waits for them, and re-layouts  53.7 us (10%)
  matrix products  48.5 us (9%)
  starting transfers between devices  20.7 us (4%)
  between operations  16.2 us (3%)
  other arithmetic  12.3 us (2%)
    unnamed x1, blocking collectives  285 us
    reduce_scatter x1, waiting for transfers between devices, per_device(): lax.psum_scatter(text_term.astype(jnp.bfloat16), 'loop', scatter_dimensio...  70.1 us
    scatter x1, local copies, waits for them, and re-layouts, per_device(): send_tokens = jnp.zeros((slot_count, crop_width, model_width), jnp.bfloat...  23.5 us
    dot_general x2, matrix products, crop_partial(): jnp.einsum('...kh,...kd->...hd', weight, tokens.astype(jnp.float32), prec...  16.9 us
    dot_general x2, matrix products, crop_partial(): jnp.dot(flat_rows, key_probe, preferred_element_type=jnp.float32)  14.5 us
    dot_general x2, matrix products, crop_partial(): jnp.einsum('...hd,dhe->...he', mixed, value_heads, precision=highest)  12.3 us
  transfers between devices with their start and end apart: 5, of which 2 were waited for; matrix products, arithmetic and copies ran while one was open for 21% of the time, Pallas kernels for 0%

profile of v1, /device:TPU:0, one launch (start us, length us, event | category | flops | bytes accessed | tf_op | source)
XLA Modules:
  0.0 510.8 jit_solution(8131910111657612544)
XLA Ops:
  7.2 0.0 copy-start
  7.2 0.9 fusion.41
  8.1 0.1 reduce_window_sum.11
  8.2 0.8 select_reduce_fusion.1
  9.0 0.7 fusion.48
  9.7 0.9 scatter_custom_fusion.1
  10.6 0.7 all_to_all.20
  11.3 6.5 %all-to-all-start.1 = ((s32[16,1,8]{2,1,0:T(1,128)}), s32[16,1,8]{2,1,0:T(1,128)S(1)}, u32[]{:S(2)}, u32[]{:S(2)}) async-start(s32[16,1,8]{2,1,0:T(1,128)} %bitcast.8), calls=%async_computation.1 | async-start | bytes 16384 | tf_op jit(solution)/shard_map/all_to_all | solution.py:128
  17.7 0.9 scatter_custom_fusion
  18.6 0.7 all_to_all.18
  19.3 4.4 all-to-all-done.1
  23.7 3.5 all-to-all-start
  27.2 7.2 %broadcast_in_dim.92 = bf16[128,64,1152]{2,1,0:T(8,128)(2,1)} broadcast(bf16[]{:T(256)} %constant.10.clone.1), dimensions={} | broadcast | bytes 18874370 | tf_op jit(solution)/shard_map/broadcast_in_dim | solution.py:116
  34.4 23.5 %scatter_fusion = bf16[128,64,1152]{2,1,0:T(8,128)(2,1)} fusion(bf16[128,64,1152]{2,1,0:T(8,128)(2,1)} %broadcast_in_dim.92, s32[64]{0:T(128)S(1)} %fusion.48, bf16[64,64,1152]{2,1,0:T(8,128)(2,1)} %param.12), kind=kCustom, calls=%fused_computation.2 | custom fusion | bytes 28311808 | tf_op jit(solution)/shard_map/scatter | solution.py:118
  57.9 5.8 %all-to-all-start.2 = ((bf16[16,8,64,1152]{3,2,1,0:T(8,128)(2,1)}), bf16[16,8,64,1152]{3,2,1,0:T(8,128)(2,1)}, u32[]{:S(2)}, u32[]{:S(2)}) async-start(bf16[16,8,64,1152]{3,2,1,0:T(8,128)(2,1)} %bitcast.61), calls=%async_computation.2 | async-start | bytes 37748736 | tf_op jit(solution)/shard_map/all_to_all | solution.py:121
  63.7 2.4 convolution_multiply_fusion.1
  66.1 0.1 reshape.119
  66.2 0.3 fusion.32
  66.5 0.1 copy.77
  66.6 0.3 fusion.33
  66.9 0.1 copy.83
  66.9 5.3 %copy.67 = bf16[1152,1152]{0,1:T(8,128)(2,1)} copy(bf16[1152,1152]{1,0:T(8,128)(2,1)} %param.18) | data formatting | bytes 5308416 | tf_op args[6]
  73.6 0.6 dynamic-slice
  74.8 0.2 dynamic-update-slice
  75.1 284.8 %all-reduce = s32[256]{0:T(256)S(1)} all-reduce(s32[256]{0:T(256)S(1)} %dynamic-update-slice), channel_id=1, replica_groups=mesh['dp'=16,'loop'=8] {'loop'}, use_global_device_ids=true, to_apply=%add | all-reduce | flops 256 | bytes 2048
  359.9 0.1 fusion.35
  360.0 4.4 fusion.34
  364.5 0.1 fusion.36
  364.6 0.5 broadcast.94
  365.1 0.7 reduce.3
  365.8 0.1 eq.51
  365.9 0.1 iota_compare_fusion
  365.9 0.0 all-to-all-done.2
  366.0 0.9 stack.2
  366.8 4.7 all-to-all-start.3
  371.6 0.2 reduce-scatter.2.cloned.1.call-start
  371.8 12.1 %convolution_multiply_fusion = f32[8192,16]{0,1:T(8,128)} fusion(bf16[8192,1152]{1,0:T(8,128)(2,1)} %bitcast.11, bf16[1152,16]{0,1:T(8,128)(2,1)S(1)} %copy-done.4), kind=kOutput, calls=%fused_computation.5 | convolution fusion | flops 302120960 | bytes 19435520 | tf_op jit(solution)/shard_map/dot_general | solution.py:19
  383.9 2.4 reshape.124
  386.4 2.0 fusion.25
  388.4 0.2 select_reduce_fusion
  388.6 0.1 copy.76
  388.7 0.1 fusion.24
  388.8 2.4 fusion.26
  391.2 0.1 copy.84
  391.3 0.9 mul.78
  392.2 2.1 copy.81
  394.3 12.4 %fusion.27 = f32[16,8,16,1152]{3,2,1,0:T(8,128)S(1)} fusion(bf16[16,8,64,1152]{3,2,1,0:T(8,128)(2,1)} %all-to-all-done.2, f32[16,8,64,16]{2,1,0,3:T(8,128)} %reshape.124, f32[16,8,16]{2,1,0:T(8,128)S(1)} %fusion.25, pred[16,8,64]{2,1,0:T(8,128)(4,1)S(1)} %iota_compare_fusion), kind=kOutput, calls=%fused_computation.33 | convolution fusion | flops 1812332544 | bytes 28852224 | tf_op jit(solution)/shard_map/...kh,...kd->...hd/dot_general | solution.py:27
  406.7 7.0 %fusion.4 = f32[16,8,16,72]{3,1,0,2:T(8,128)S(1)} fusion(bf16[1152,16,72,1]{0,2,3,1:T(8,128)(2,1)S(1)} %bitcast.63, f32[16,8,16,1152]{3,2,1,0:T(8,128)S(1)} %fusion.27), kind=kOutput, calls=%fused_computation.9 | convolution fusion | flops 2038431744 | bytes 12681216 | tf_op jit(solution)/shard_map/...hd,dhe->...he/dot_general | solution.py:29
  413.7 1.6 copy.79
  415.3 2.5 reshape_reshape_reshape.3
  417.8 2.1 multiply_bitcast_fusion
  419.9 2.1 copy.82
  422.0 0.1 convolution_add_fusion.1
  422.1 5.3 %fusion.10 = f32[32,16,72]{2,0,1:T(8,128)S(1)} fusion(bf16[1152,16,72]{0,2,1:T(8,128)(2,1)} %bitcast.62, f32[32,16,1152]{2,1,0:T(8,128)} %fusion.34, f32[32,16]{0,1:T(8,128)S(1)} %subtract_exponential_fusion), kind=kOutput, calls=%fused_computation.11 | convolution fusion | flops 509644800 | bytes 5163008 | tf_op jit(solution)/shard_map/...hd,dhe->...he/dot_general | solution.py:29
  427.4 0.9 fusion.14
  428.3 0.1 copy.85
  428.4 0.2 convert_element_type.37
  428.5 1.3 multiply_reduce_fusion
  429.9 0.3 fusion.23
  430.2 1.2 convolution_convert_fusion
  431.4 0.0 reduce-scatter.2.cloned.1.call-update
  431.4 0.9 fusion.57
  432.3 70.1 %reduce-scatter.2.cloned.1.call-done = bf16[32,1152]{1,0:T(8,128)(2,1)} async-done(((bf16[256,1152]{1,0:T(8,128)(2,1)}), bf16[32,1152]{1,0:T(8,128)(2,1)}) %reduce-scatter.2.cloned.1.call-update) | async-done | bytes 73744 | tf_op jit(solution)/shard_map/reduce_scatter | solution.py:158
  502.4 1.6 convert_element_type.44
  (22 shorter events, 0.1 us)
Async XLA Ops:
  7.2 421.4 %copy-start = (bf16[1152,1152]{1,0:T(8,128)(2,1)S(1)}, bf16[1152,1152]{1,0:T(8,128)(2,1)}, u32[]{:S(2)}) copy-start(bf16[1152,1152]{1,0:T(8,128)(2,1)} %param.19) | copy-start | bytes 7962628
  11.3 12.5 %all-to-all-start.1 = ((s32[16,1,8]{2,1,0:T(1,128)}), s32[16,1,8]{2,1,0:T(1,128)S(1)}, u32[]{:S(2)}, u32[]{:S(2)}) async-start(s32[16,1,8]{2,1,0:T(1,128)} %bitcast.8), calls=%async_computation.1 | async-start | bytes 16384 | tf_op jit(solution)/shard_map/all_to_all | solution.py:128
  23.7 34.1 %all-to-all-start = ((s32[16,1,8]{2,1,0:T(1,128)}), s32[16,1,8]{2,1,0:T(1,128)S(1)}, u32[]{:S(2)}, u32[]{:S(2)}) async-start(s32[16,1,8]{2,1,0:T(1,128)} %bitcast.6), calls=%async_computation | async-start | bytes 16384 | tf_op jit(solution)/shard_map/all_to_all | solution.py:131
  57.9 5.8 %copy-start.4 = (bf16[1152,16]{0,1:T(8,128)(2,1)S(1)}, bf16[1152,16]{0,1:T(8,128)(2,1)}, u32[]{:S(2)}) copy-start(bf16[1152,16]{0,1:T(8,128)(2,1)} %param.17) | copy-start | bytes 110596
  57.9 308.1 %all-to-all-start.2 = ((bf16[16,8,64,1152]{3,2,1,0:T(8,128)(2,1)}), bf16[16,8,64,1152]{3,2,1,0:T(8,128)(2,1)}, u32[]{:S(2)}, u32[]{:S(2)}) async-start(bf16[16,8,64,1152]{3,2,1,0:T(8,128)(2,1)} %bitcast.61), calls=%async_computation.2 | async-start | bytes 37748736 | tf_op jit(solution)/shard_map/all_to_all | solution.py:121
  66.9 6.6 %copy-start.6 = (u32[128]{0:T(128)S(1)}, u32[128]{0:T(128)}, u32[]{:S(2)}) copy-start(u32[128]{0:T(128)} %constant.46) | copy-start | bytes 1540
  66.9 7.9 %copy-start.5 = (s32[32]{0:T(128)S(1)}, s32[32]{0:T(128)}, u32[]{:S(2)}) copy-start(s32[32]{0:T(128)} %param.21) | copy-start | bytes 388
  66.9 293.0 %copy-start.3 = (bf16[32,1152]{1,0:T(8,128)(2,1)S(1)}, bf16[32,1152]{1,0:T(8,128)(2,1)}, u32[]{:S(2)}) copy-start(bf16[32,1152]{1,0:T(8,128)(2,1)} %param.20) | copy-start | bytes 221188
  366.8 63.1 %all-to-all-start.3 = ((bf16[8,32,1152]{2,1,0:T(8,128)(2,1)}), bf16[8,32,1152]{2,1,0:T(8,128)(2,1)S(1)}, u32[]{:S(2)}, u32[]{:S(2)}) async-start(bf16[8,32,1152]{2,1,0:T(8,128)(2,1)} %stack.2), calls=%async_computation.3 | async-start | bytes 1179648 | tf_op jit(solution)/shard_map/all_to_all | solution.py:152
  371.6 130.8 %reduce-scatter.2.cloned.1.call-start = ((), (), s32[]{:S(2)}) async-start(), calls=%async_computation.5 | async-start | bytes 663552 | tf_op jit(solution)/shard_map/reduce_scatter | solution.py:158
  394.3 12.5 %copy-start.1 = (bf16[1152,1152]{0,1:T(8,128)(2,1)S(1)}, bf16[1152,1152]{0,1:T(8,128)(2,1)}, u32[]{:S(2)}) copy-start(bf16[1152,1152]{0,1:T(8,128)(2,1)} %copy.67) | copy-start | bytes 7962628
  422.1 5.3 %copy-start.2 = (f32[1152,128]{1,0:T(8,128)S(1)}, f32[1152,128]{1,0:T(8,128)}, u32[]{:S(2)}) copy-start(f32[1152,128]{1,0:T(8,128)} %copy.82) | copy-start | bytes 1769476
Sparse Core Ops, SparseCore 0:
  431.5 70.8 reduce-scatter.1
